TPU v7x, 32 devices: a whole 2x2x4 slice. The times are simulated.
32 devices in a mesh: col: 4 (over z), row: 8 (over y, x, core).
Axes of the slice: x: 2, y: 2, z: 4, core: 2. Of those that a mesh axis runs over, the one named last changes fastest.
Arguments:
- affinity: bfloat16 [3840, 128, 128], P(('col', 'row')), may hold values from 0 to 0.015625
- tile_rows: int32 [3840], P(('col', 'row')), may hold values from 0 to 19
- tile_cols: int32 [3840], P(('col', 'row')), may hold values from 0 to 39
- live_tiles: int32 [32], P(('col', 'row')), may hold values from 1 to 120, as said below
- start: float32 [20480, 256], P(('col', 'row')), may hold values from -1500 to 1500
Outputs:
- vectors: float32 [20480, 256], P(('col', 'row'))
- first_passes: float32 [2, 20480, 256], P(None, ('col', 'row'))
Inputs may be any that keep to these rules, and one draw needn't show every extreme that they name: A device's tiles are its slots 0 to live_tiles - 1; later slots are ignored. Some device holds exactly 120 tiles.
All inputs are finite; a program needn't handle non-finite values.
Results may differ from a plain program's by a relative error of at most 0.0003.
Values sent between devices are 32-bit elements; how exact they have to be, the bound alone decides.
No kernel may reach another device: no remote copies, remote signals or barrier semaphores. Data moves between devices by JAX's collectives and lax.ppermute only.
A program may use at most 128 MiB of HBM per device.

v0:
```python
import jax
import jax.numpy as jnp
from jax import lax
from jax.sharding import PartitionSpec as P

ITERS = 2
highest = lax.Precision.HIGHEST


def local_gram(matrix):
    return jnp.dot(matrix.T, matrix, precision=highest, preferred_element_type=jnp.float32)


def inverse_lower(gram):
    lower = jnp.linalg.cholesky(gram)
    return jax.scipy.linalg.solve_triangular(
        lower, jnp.eye(gram.shape[0], dtype=jnp.float32), lower=True
    )


def apply_factor(matrix, inverse):
    return jnp.dot(matrix, inverse.T, precision=highest, preferred_element_type=jnp.float32)


def body(affinity, tile_rows, tile_cols, live_tiles, start):
    n_row = lax.axis_size("row")
    n_col = lax.axis_size("col")
    slot_count = affinity.shape[0]
    tile_size = affinity.shape[1]
    rows_local = start.shape[0]
    vec_count = start.shape[1]
    own_tiles = rows_local // tile_size
    live = (jnp.arange(slot_count) < live_tiles[0]).astype(jnp.float32)
    row_onehot = (jnp.arange(own_tiles * n_col)[:, None] == tile_rows[None, :]).astype(
        jnp.float32
    ) * live[None, :]
    row_sums = jnp.sum(affinity, axis=2, dtype=jnp.float32)
    degree_terms = jnp.dot(
        row_onehot, row_sums, precision=highest, preferred_element_type=jnp.float32
    )
    degree = 1.0 + lax.psum_scatter(degree_terms, "col", scatter_dimension=0, tiled=True).reshape(
        rows_local
    )
    scaling = (1.0 / jnp.sqrt(degree))[:, None]
    squares = affinity.astype(jnp.float32)
    firsts = []
    pending = start
    for step_number in range(ITERS):
        mapped_scaled = scaling * pending
        gathered = lax.all_gather(mapped_scaled, "row", axis=0, tiled=True)
        gathered = gathered.reshape(n_row * own_tiles, tile_size, vec_count)
        picked = gathered[tile_cols]
        products = jnp.einsum(
            "sij,sjk->sik", squares, picked, precision=highest, preferred_element_type=jnp.float32
        )
        terms = jnp.dot(
            row_onehot,
            products.reshape(slot_count, tile_size * vec_count),
            precision=highest,
            preferred_element_type=jnp.float32,
        )
        summed = lax.psum_scatter(terms, "col", scatter_dimension=0, tiled=True)
        raw_image = scaling * (mapped_scaled + summed.reshape(rows_local, vec_count))
        if step_number == 0:
            inner_gram = lax.psum(local_gram(raw_image), ("col", "row"))
            image_block = raw_image
        else:
            raw_gram, pending_gram = lax.psum(
                (local_gram(raw_image), local_gram(pending)), ("col", "row")
            )
            pending_inverse = inverse_lower(pending_gram)
            image_block = apply_factor(raw_image, pending_inverse)
            inner_gram = jnp.dot(
                jnp.dot(
                    pending_inverse, raw_gram, precision=highest, preferred_element_type=jnp.float32
                ),
                pending_inverse.T,
                precision=highest,
                preferred_element_type=jnp.float32,
            )
        pending = apply_factor(image_block, inverse_lower(inner_gram))
        firsts.append(pending)
    final_gram = lax.psum(local_gram(pending), ("col", "row"))
    basis = apply_factor(pending, inverse_lower(final_gram))
    total_images = rows_local * n_row * n_col
    root = jnp.sqrt(jnp.float32(total_images))
    return (root * basis, root * jnp.stack(firsts, axis=0))


def solution(mesh):
    placed = (
        P(("col", "row"), None, None),
        P(("col", "row")),
        P(("col", "row")),
        P(("col", "row")),
        P(("col", "row"), None),
    )
    return jax.shard_map(
        body,
        mesh=mesh,
        in_specs=placed,
        out_specs=(P(("col", "row"), None), P(None, ("col", "row"), None)),
        check_vma=False,
    )
```

profile of v0, /device:TPU:0, one launch (start us, length us, event | category | flops | bytes accessed | tf_op | source)
XLA Modules:
  0.0 1157.0 jit_solution(773065271221598994)
XLA Ops:
  7.9 3.2 convert_reduce_fusion
  11.9 20.4 %all-reduce.1 = f32[20,128]{1,0:T(8,128)S(1)} all-reduce(f32[20,128]{1,0:T(8,128)S(1)} %fusion.55), channel_id=2, replica_groups=mesh['col'=4,'row'=8] {'col'}, use_global_device_ids=true, to_apply=%region_1.0.clone | all-reduce | flops 2560 | bytes 20480
  34.4 2.1 broadcast_multiply_fusion.1
  36.6 39.3 %all-gather.3.cloned.1.call-done = f32[5120,256]{1,0:T(8,128)} async-done(((f32[640,256]{1,0:T(8,128)}), f32[5120,256]{1,0:T(8,128)}) %all-gather.3.cloned.1.call-update) | async-done | bytes 5242896 | tf_op jit(solution)/shard_map/all_gather | solution.py:50
  75.9 12.1 %gather_fusion = f32[120,128,256]{2,1,0:T(8,128)} fusion(f32[40,128,256]{2,1,0:T(8,128)} %bitcast.166, s32[1024]{0:T(1024)S(1)} %pad_clamp_fusion), kind=kCustom, calls=%fused_computation | custom fusion | bytes 31457760 | tf_op jit(solution)/shard_map/gather | solution.py:52
  88.0 20.2 %convolution_bitcast_fusion.1 = f32[120,128,256]{1,2,0:T(8,128)} fusion(f32[120,128,256]{2,1,0:T(8,128)} %gather_fusion, bf16[120,128,128]{2,1,0:T(8,128)(2,1)} %param.8), kind=kOutput, calls=%fused_computation.11 | convolution fusion | flops 6039797760 | bytes 35389440 | tf_op jit(solution)/shard_map/sij,sjk->sik/dot_general | solution.py:53
  108.2 15.7 %copy.41 = f32[15,8,128,256]{3,1,2,0:T(8,128)} copy(f32[15,8,128,256]{2,3,1,0:T(8,128)} %bitcast.163) | data formatting | bytes 31457280
  123.9 10.5 fusion.53
  134.4 78.5 %fusion = f32[8,32768]{1,0:T(8,128)} fusion(f32[20,32768]{1,0:T(8,128)S(1)} %fusion.53), kind=kCustom, calls=%all-reduce-scatter | all-reduce-scatter fusion | flops 1048577 | bytes 3670528
  215.7 2.6 collective-permute-start.1
  219.0 20.1 %collective-permute-done.1 = f32[1,32768]{1,0:T(1,128)S(1)} collective-permute-done((f32[1,32768]{1,0:T(1,128)S(1)}, f32[1,32768]{1,0:T(1,128)S(1)}, u32[]{:S(2)}, u32[]{:S(2)}) %collective-permute-start.1) | collective-permute-done | bytes 131104
  239.1 21.2 %concatenate.3 = f32[17,32768]{1,0:T(8,128)} concatenate(f32[1,32768]{1,0:T(1,128)S(1)} %collective-permute-done.1, f32[8,32768]{1,0:T(8,128)S(1)} %collective-permute-done, f32[8,32768]{1,0:T(8,128)} %fusion), dimensions={0} | concatenate | bytes 4456448
  262.4 2.2 fusion.29
  264.6 129.0 %all-reduce.11.cloned.1.call-done = f32[256,256]{0,1:T(8,128)} async-done(((f32[256,256]{0,1:T(8,128)}), f32[256,256]{0,1:T(8,128)}) %all-reduce.11.cloned.1.call-update) | async-done | bytes 262160 | tf_op jit(solution)/shard_map/psum | solution.py:65
  395.7 11.7 %cholesky.214 = f32[128,128]{1,0:T(8,128)S(1)} custom-call(f32[128,128]{1,0:T(8,128)S(1)} %cholesky.346), custom_call_target="Cholesky" | custom-call | tf_op jit(solution)/shard_map/jit(cholesky)/cholesky | solution.py:15
  407.5 9.8 custom-call.17
  417.8 11.7 %cholesky.231 = f32[128,128]{1,0:T(8,128)S(1)} custom-call(f32[128,128]{1,0:T(8,128)S(1)} %convolution_subtract_fusion.7), custom_call_target="Cholesky" | custom-call | tf_op jit(solution)/shard_map/jit(cholesky)/cholesky | solution.py:15
  431.8 15.1 %while.8 = (s32[]{:T(128)}, f32[256,256]{1,0:T(8,128)S(1)}, s32[2,2]{1,0:T(2,128)S(1)}, f32[2,128,128]{2,1,0:T(8,128)S(1)}, s32[]{:T(128)}) while((s32[]{:T(128)}, f32[256,256]{1,0:T(8,128)S(1)}, s32[2,2]{1,0:T(2,128)S(1)}, f32[2,128,128]{2,1,0:T(8,128)S(1)}, s32[]{:T(128)}) %tuple.83), condition=%wide.while_cond, body=%wide.while_body.sunk | while | flops 2 | bytes 131181 | solution.py:16
  446.9 19.7 %custom-call.18 = f32[2,128,128]{1,2,0:T(8,128)S(1)} custom-call(f32[2,128,128]{2,1,0:T(8,128)S(1)} %get-tuple-element.30), custom_call_target="InvertDiagBlocksLowerTriangular" | custom-call | tf_op jit(solution)/shard_map/jit(_solve_triangular)/triangular_solve | solution.py:16
  469.1 40.2 %all-gather.5.cloned.1.call-done = f32[5120,256]{1,0:T(8,128)} async-done(((f32[640,256]{1,0:T(8,128)}), f32[5120,256]{1,0:T(8,128)}) %all-gather.5.cloned.1.call-update) | async-done | bytes 5242896 | tf_op jit(solution)/shard_map/all_gather | solution.py:50
  509.3 12.1 %gather_fusion.1 = f32[120,128,256]{2,1,0:T(8,128)} fusion(f32[40,128,256]{2,1,0:T(8,128)} %bitcast.167, s32[1024]{0:T(1024)S(1)} %pad_clamp_fusion), kind=kCustom, calls=%fused_computation.1 | custom fusion | bytes 31457760 | tf_op jit(solution)/shard_map/gather | solution.py:52
  521.4 20.2 %convolution_bitcast_fusion = f32[120,128,256]{1,2,0:T(8,128)} fusion(f32[120,128,256]{2,1,0:T(8,128)} %gather_fusion.1, bf16[120,128,128]{2,1,0:T(8,128)(2,1)} %param.8), kind=kOutput, calls=%fused_computation.10 | convolution fusion | flops 6039797760 | bytes 35389440 | tf_op jit(solution)/shard_map/sij,sjk->sik/dot_general | solution.py:53
  541.6 15.7 %copy.42 = f32[15,8,128,256]{3,1,2,0:T(8,128)} copy(f32[15,8,128,256]{2,3,1,0:T(8,128)} %bitcast.165) | data formatting | bytes 31457280
  557.3 11.6 fusion.51
  568.9 78.6 %fusion.1 = f32[8,32768]{1,0:T(8,128)S(1)} fusion(f32[20,32768]{1,0:T(8,128)} %fusion.51), kind=kCustom, calls=%all-reduce-scatter.1 | all-reduce-scatter fusion | flops 1048577 | bytes 3670528
  647.4 2.3 collective-permute-start.2
  651.5 1.9 fusion.82
  653.4 19.9 %collective-permute-done.3 = f32[1,32768]{1,0:T(1,128)S(1)} collective-permute-done((f32[1,32768]{1,0:T(1,128)S(1)}, f32[1,32768]{1,0:T(1,128)S(1)}, u32[]{:S(2)}, u32[]{:S(2)}) %collective-permute-start.3) | collective-permute-done | bytes 131104
  673.3 21.2 %concatenate.4 = f32[17,32768]{1,0:T(8,128)} concatenate(f32[1,32768]{1,0:T(1,128)S(1)} %collective-permute-done.3, f32[8,32768]{1,0:T(8,128)} %collective-permute-done.2, f32[8,32768]{1,0:T(8,128)S(1)} %fusion.1), dimensions={0} | concatenate | bytes 4456448
  696.6 2.1 fusion.30
  698.8 131.3 %all-reduce.15.cloned.1.call-done = (f32[256,256]{0,1:T(8,128)}, f32[256,256]{1,0:T(8,128)}) async-done(((f32[256,256]{0,1:T(8,128)}, f32[256,256]{1,0:T(8,128)}), (f32[256,256]{0,1:T(8,128)}, f32[256,256]{1,0:T(8,128)})) %all-reduce.15.cloned.1.call-update) | async-done | bytes 524304 | tf_op jit(solution)/shard_map/psum | solution.py:68
  832.2 11.7 %cholesky.248 = f32[128,128]{1,0:T(8,128)S(1)} custom-call(f32[128,128]{1,0:T(8,128)S(1)} %cholesky.349), custom_call_target="Cholesky" | custom-call | tf_op jit(solution)/shard_map/jit(cholesky)/cholesky | solution.py:15
  844.0 9.8 custom-call.19
  854.3 11.7 %cholesky.265 = f32[128,128]{1,0:T(8,128)S(1)} custom-call(f32[128,128]{1,0:T(8,128)S(1)} %convolution_subtract_fusion.6), custom_call_target="Cholesky" | custom-call | tf_op jit(solution)/shard_map/jit(cholesky)/cholesky | solution.py:15
  868.7 4.0 while.9
  872.7 19.8 %custom-call.20 = f32[2,128,128]{1,2,0:T(8,128)S(1)} custom-call(f32[2,128,128]{2,1,0:T(8,128)S(1)} %get-tuple-element.31), custom_call_target="InvertDiagBlocksLowerTriangular" | custom-call | tf_op jit(solution)/shard_map/jit(_solve_triangular)/triangular_solve | solution.py:16
  895.2 11.7 %cholesky.282 = f32[128,128]{1,0:T(8,128)S(1)} custom-call(f32[128,128]{1,0:T(8,128)S(1)} %cholesky.352), custom_call_target="Cholesky" | custom-call | tf_op jit(solution)/shard_map/jit(cholesky)/cholesky | solution.py:15
  907.0 9.8 custom-call.21
  917.3 11.9 %cholesky.299 = f32[128,128]{1,0:T(8,128)S(1)} custom-call(f32[128,128]{1,0:T(8,128)S(1)} %convolution_subtract_fusion.5), custom_call_target="Cholesky" | custom-call | tf_op jit(solution)/shard_map/jit(cholesky)/cholesky | solution.py:15
  931.8 4.0 while.10
  935.8 19.7 %custom-call.22 = f32[2,128,128]{1,2,0:T(8,128)S(1)} custom-call(f32[2,128,128]{2,1,0:T(8,128)S(1)} %get-tuple-element.32), custom_call_target="InvertDiagBlocksLowerTriangular" | custom-call | tf_op jit(solution)/shard_map/jit(_solve_triangular)/triangular_solve | solution.py:16
  957.2 1.9 fusion.83
  960.3 124.6 %all-reduce.13.cloned.1.call-done = f32[256,256]{0,1:T(8,128)} async-done(((f32[256,256]{0,1:T(8,128)}), f32[256,256]{0,1:T(8,128)}) %all-reduce.13.cloned.1.call-update) | async-done | bytes 262160 | tf_op jit(solution)/shard_map/psum | solution.py:83
  1087.0 11.7 %cholesky.316 = f32[128,128]{1,0:T(8,128)S(1)} custom-call(f32[128,128]{1,0:T(8,128)S(1)} %cholesky.355), custom_call_target="Cholesky" | custom-call | tf_op jit(solution)/shard_map/jit(cholesky)/cholesky | solution.py:15
  1098.8 9.8 custom-call.23
  1109.1 11.9 %cholesky.333 = f32[128,128]{1,0:T(8,128)S(1)} custom-call(f32[128,128]{1,0:T(8,128)S(1)} %convolution_subtract_fusion.4), custom_call_target="Cholesky" | custom-call | tf_op jit(solution)/shard_map/jit(cholesky)/cholesky | solution.py:15
  1123.8 4.1 while.11
  1127.9 19.7 %custom-call.24 = f32[2,128,128]{1,2,0:T(8,128)S(1)} custom-call(f32[2,128,128]{2,1,0:T(8,128)S(1)} %get-tuple-element.33), custom_call_target="InvertDiagBlocksLowerTriangular" | custom-call | tf_op jit(solution)/shard_map/jit(_solve_triangular)/triangular_solve | solution.py:16
  (127 shorter events, 50.9 us)
Async XLA Ops:
  7.2 29.4 %copy-start.3 = (s32[120]{0:T(128)S(1)}, s32[120]{0:T(128)}, u32[]{:S(2)}) copy-start(s32[120]{0:T(128)} %param.10) | copy-start | bytes 1444
  7.2 68.7 %all-gather.3.cloned.1.call-start = ((), (), s32[]{:S(2)}) async-start(), calls=%async_computation | async-start | bytes 5898240 | tf_op jit(solution)/shard_map/all_gather | solution.py:50
  36.5 357.1 %all-reduce.11.cloned.1.call-start = ((), (), s32[]{:S(2)}) async-start(), calls=%async_computation.1 | async-start | bytes 524288 | tf_op jit(solution)/shard_map/psum | solution.py:65
  108.2 15.7 %copy-start.2 = (s32[120]{0:T(128)S(1)}, s32[120]{0:T(128)}, u32[]{:S(2)}) copy-start(s32[120]{0:T(128)} %param.9) | copy-start | bytes 1444
  212.9 49.5 %copy-start = (f32[640,256]{1,0:T(8,128)S(1)}, f32[640,256]{1,0:T(8,128)}, u32[]{:S(2)}) copy-start(f32[640,256]{1,0:T(8,128)} %param.12) | copy-start | bytes 1966084
  212.9 26.2 %collective-permute-start = (f32[8,32768]{1,0:T(8,128)}, f32[8,32768]{1,0:T(8,128)S(1)}, u32[]{:S(2)}, u32[]{:S(2)}) collective-permute-start(f32[8,32768]{1,0:T(8,128)} %fusion), channel_id=1, source_target_pairs={{0,8},{8,16},{16,24},{1,9},{9,17},{17,25},{2,10},{10,18},{18,26},{... | collective-permute-start | bytes 3145736
  215.7 23.4 %collective-permute-start.1 = (f32[1,32768]{1,0:T(1,128)S(1)}, f32[1,32768]{1,0:T(1,128)S(1)}, u32[]{:S(2)}, u32[]{:S(2)}) collective-permute-start(f32[1,32768]{1,0:T(1,128)S(1)} %slice.54), channel_id=1, source_target_pairs={{0,16},{8,24},{1,17},{9,25},{2,18},{10,26},{3,19},{11,27},{4,20},{... | collective-permute-start | bytes 393224
  264.6 244.7 %all-gather.5.cloned.1.call-start = ((), (), s32[]{:S(2)}) async-start(), calls=%async_computation.2 | async-start | bytes 5898240 | tf_op jit(solution)/shard_map/all_gather | solution.py:50
  469.1 361.0 %all-reduce.15.cloned.1.call-start = ((), (), s32[]{:S(2)}) async-start(), calls=%async_computation.4 | async-start | bytes 1048576 | tf_op jit(solution)/shard_map/psum | solution.py:68
  647.4 25.9 %collective-permute-start.2 = (f32[8,32768]{1,0:T(8,128)S(1)}, f32[8,32768]{1,0:T(8,128)}, u32[]{:S(2)}, u32[]{:S(2)}) collective-permute-start(f32[8,32768]{1,0:T(8,128)S(1)} %fusion.1), channel_id=1, source_target_pairs={{0,8},{8,16},{16,24},{1,9},{9,17},{17,25},{2,10},{10,18},{18,26},{... | collective-permute-start | bytes 3145736
  649.8 23.5 %collective-permute-start.3 = (f32[1,32768]{1,0:T(1,128)S(1)}, f32[1,32768]{1,0:T(1,128)S(1)}, u32[]{:S(2)}, u32[]{:S(2)}) collective-permute-start(f32[1,32768]{1,0:T(1,128)S(1)} %slice.55), channel_id=1, source_target_pairs={{0,16},{8,24},{1,17},{9,25},{2,18},{10,26},{3,19},{11,27},{4,20},{... | collective-permute-start | bytes 393224
  698.7 386.2 %all-reduce.13.cloned.1.call-start = ((), (), s32[]{:S(2)}) async-start(), calls=%async_computation.3 | async-start | bytes 524288 | tf_op jit(solution)/shard_map/psum | solution.py:83
  830.1 64.1 %copy-start.1 = (f32[256,256]{1,0:T(8,128)S(1)}, f32[256,256]{1,0:T(8,128)}, u32[]{:S(2)}) copy-start(f32[256,256]{1,0:T(8,128)} %get-tuple-element.67) | copy-start | bytes 786436
Sparse Core Ops, SparseCore 0:
  36.7 39.1 all-gather.2
  264.7 128.9 all-reduce.10
  469.2 40.0 all-gather.4
  698.9 131.1 all-reduce.14
  959.2 125.6 all-reduce.12
where the time goes:
time: 1170 us; the launch traced here: 1160 us
  waiting for transfers between devices  504 us (43%)
  other arithmetic  227 us (19%)
  blocking collectives  177 us (15%)
  local copies, waits for them, and re-layouts  125 us (11%)
  matrix products  82.1 us (7%)
  between operations  22.1 us (2%)
    unnamed x3, blocking collectives  177 us
    another operation x27, other arithmetic, inverse_lower(): lower = jnp.linalg.cholesky(gram)  138 us
    psum x1, waiting for transfers between devices, body(): lax.psum((local_gram(raw_image), local_gram(pending)), ('col', 'row'))  131 us
    psum x1, waiting for transfers between devices, body(): inner_gram = lax.psum(local_gram(raw_image), ('col', 'row'))  129 us
    psum x1, waiting for transfers between devices, body(): final_gram = lax.psum(local_gram(pending), ('col', 'row'))  125 us
    unnamed x17, local copies, waits for them, and re-layouts  80.2 us
    all_gather x2, waiting for transfers between devices, body(): gathered = lax.all_gather(mapped_scaled, 'row', axis=0, tiled=True)  79.4 us
    another operation x9, other arithmetic, inverse_lower(): jax.scipy.linalg.solve_triangular(lower, jnp.eye(gram.shape[0], dtype=jnp...  79 us
  transfers between devices with their start and end apart: 9, of which 7 were waited for; matrix products, arithmetic and copies ran while one was open for 0% of the time, Pallas kernels for 0%

commit v1 on v0

--- a/solution.py
+++ b/solution.py
@@ -80,7 +80,7 @@
             )
         pending = apply_factor(image_block, inverse_lower(inner_gram))
         firsts.append(pending)
-    final_gram = lax.psum(local_gram(pending), ("col", "row"))
+    final_gram = lax.psum(lax.psum(local_gram(pending), "col"), "row")
     basis = apply_factor(pending, inverse_lower(final_gram))
     total_images = rows_local * n_row * n_col
     root = jnp.sqrt(jnp.float32(total_images))

time: 1170 us -> 1130 us (0.966)
  waiting for transfers between devices: 504 us -> 470 us
    psum x1 -> x2, waiting for transfers between devices: 125 us -> 90.2 us  [body(): final_gram = lax.psum(lax.psum(local_gram(pending), 'col'), 'row')]
    unnamed x9 -> x10, waiting for transfers between devices: 40 us -> 40 us
  transfers between devices with their start and end apart: 9 -> 10, of which waited for: 7 -> 8; matrix products, arithmetic and copies ran while one was open for 0% -> 0% of each run, Pallas kernels for 0% -> 0%
where the time goes in v1:
time: 1130 us; the launch traced here: 1120 us
  waiting for transfers between devices  470 us (42%)
  other arithmetic  227 us (20%)
  blocking collectives  177 us (16%)
  local copies, waits for them, and re-layouts  125 us (11%)
  matrix products  82.1 us (7%)
  between operations  22.4 us (2%)
  loops' own time  11.5 us (1%)
    unnamed x3, blocking collectives  177 us
    another operation x27, other arithmetic, inverse_lower(): lower = jnp.linalg.cholesky(gram)  138 us
    psum x1, waiting for transfers between devices, body(): lax.psum((local_gram(raw_image), local_gram(pending)), ('col', 'row'))  131 us
    psum x1, waiting for transfers between devices, body(): inner_gram = lax.psum(local_gram(raw_image), ('col', 'row'))  129 us
    psum x2, waiting for transfers between devices, body(): final_gram = lax.psum(lax.psum(local_gram(pending), 'col'), 'row')  90.2 us
    unnamed x17, local copies, waits for them, and re-layouts  80.2 us
    all_gather x2, waiting for transfers between devices, body(): gathered = lax.all_gather(mapped_scaled, 'row', axis=0, tiled=True)  79.4 us
    another operation x9, other arithmetic, inverse_lower(): jax.scipy.linalg.solve_triangular(lower, jnp.eye(gram.shape[0], dtype=jnp...  79 us
  transfers between devices with their start and end apart: 10, of which 8 were waited for; matrix products, arithmetic and copies ran while one was open for 0% of the time, Pallas kernels for 0%

profile of v1, /device:TPU:0, one launch (start us, length us, event | category | flops | bytes accessed | tf_op | source)
XLA Modules:
  0.0 1123.0 jit_solution(1473005426352865048)
XLA Ops:
  7.9 3.2 convert_reduce_fusion
  11.9 20.4 %all-reduce.1 = f32[20,128]{1,0:T(8,128)S(1)} all-reduce(f32[20,128]{1,0:T(8,128)S(1)} %fusion.55), channel_id=2, replica_groups=mesh['col'=4,'row'=8] {'col'}, use_global_device_ids=true, to_apply=%region_1.0.clone | all-reduce | flops 2560 | bytes 20480
  34.4 2.1 broadcast_multiply_fusion.1
  36.6 39.3 %all-gather.3.cloned.1.call-done = f32[5120,256]{1,0:T(8,128)} async-done(((f32[640,256]{1,0:T(8,128)}), f32[5120,256]{1,0:T(8,128)}) %all-gather.3.cloned.1.call-update) | async-done | bytes 5242896 | tf_op jit(solution)/shard_map/all_gather | solution.py:50
  75.9 12.1 %gather_fusion = f32[120,128,256]{2,1,0:T(8,128)} fusion(f32[40,128,256]{2,1,0:T(8,128)} %bitcast.166, s32[1024]{0:T(1024)S(1)} %pad_clamp_fusion), kind=kCustom, calls=%fused_computation | custom fusion | bytes 31457760 | tf_op jit(solution)/shard_map/gather | solution.py:52
  88.0 20.2 %convolution_bitcast_fusion.1 = f32[120,128,256]{1,2,0:T(8,128)} fusion(f32[120,128,256]{2,1,0:T(8,128)} %gather_fusion, bf16[120,128,128]{2,1,0:T(8,128)(2,1)} %param.8), kind=kOutput, calls=%fused_computation.11 | convolution fusion | flops 6039797760 | bytes 35389440 | tf_op jit(solution)/shard_map/sij,sjk->sik/dot_general | solution.py:53
  108.2 15.7 %copy.41 = f32[15,8,128,256]{3,1,2,0:T(8,128)} copy(f32[15,8,128,256]{2,3,1,0:T(8,128)} %bitcast.163) | data formatting | bytes 31457280
  123.9 10.5 fusion.53
  134.4 78.5 %fusion = f32[8,32768]{1,0:T(8,128)} fusion(f32[20,32768]{1,0:T(8,128)S(1)} %fusion.53), kind=kCustom, calls=%all-reduce-scatter | all-reduce-scatter fusion | flops 1048577 | bytes 3670528
  215.7 2.6 collective-permute-start.1
  219.0 20.1 %collective-permute-done.1 = f32[1,32768]{1,0:T(1,128)S(1)} collective-permute-done((f32[1,32768]{1,0:T(1,128)S(1)}, f32[1,32768]{1,0:T(1,128)S(1)}, u32[]{:S(2)}, u32[]{:S(2)}) %collective-permute-start.1) | collective-permute-done | bytes 131104
  239.1 21.2 %concatenate.3 = f32[17,32768]{1,0:T(8,128)} concatenate(f32[1,32768]{1,0:T(1,128)S(1)} %collective-permute-done.1, f32[8,32768]{1,0:T(8,128)S(1)} %collective-permute-done, f32[8,32768]{1,0:T(8,128)} %fusion), dimensions={0} | concatenate | bytes 4456448
  262.4 2.2 fusion.29
  264.6 129.0 %all-reduce.12.cloned.1.call-done = f32[256,256]{0,1:T(8,128)} async-done(((f32[256,256]{0,1:T(8,128)}), f32[256,256]{0,1:T(8,128)}) %all-reduce.12.cloned.1.call-update) | async-done | bytes 262160 | tf_op jit(solution)/shard_map/psum | solution.py:65
  395.7 11.7 %cholesky.214 = f32[128,128]{1,0:T(8,128)S(1)} custom-call(f32[128,128]{1,0:T(8,128)S(1)} %cholesky.346), custom_call_target="Cholesky" | custom-call | tf_op jit(solution)/shard_map/jit(cholesky)/cholesky | solution.py:15
  407.5 9.8 custom-call.17
  417.8 11.7 %cholesky.231 = f32[128,128]{1,0:T(8,128)S(1)} custom-call(f32[128,128]{1,0:T(8,128)S(1)} %convolution_subtract_fusion.7), custom_call_target="Cholesky" | custom-call | tf_op jit(solution)/shard_map/jit(cholesky)/cholesky | solution.py:15
  431.8 15.1 %while.8 = (s32[]{:T(128)}, f32[256,256]{1,0:T(8,128)S(1)}, s32[2,2]{1,0:T(2,128)S(1)}, f32[2,128,128]{2,1,0:T(8,128)S(1)}, s32[]{:T(128)}) while((s32[]{:T(128)}, f32[256,256]{1,0:T(8,128)S(1)}, s32[2,2]{1,0:T(2,128)S(1)}, f32[2,128,128]{2,1,0:T(8,128)S(1)}, s32[]{:T(128)}) %tuple.83), condition=%wide.while_cond, body=%wide.while_body.sunk | while | flops 2 | bytes 131181 | solution.py:16
  446.9 19.7 %custom-call.18 = f32[2,128,128]{1,2,0:T(8,128)S(1)} custom-call(f32[2,128,128]{2,1,0:T(8,128)S(1)} %get-tuple-element.30), custom_call_target="InvertDiagBlocksLowerTriangular" | custom-call | tf_op jit(solution)/shard_map/jit(_solve_triangular)/triangular_solve | solution.py:16
  469.1 40.2 %all-gather.5.cloned.1.call-done = f32[5120,256]{1,0:T(8,128)} async-done(((f32[640,256]{1,0:T(8,128)}), f32[5120,256]{1,0:T(8,128)}) %all-gather.5.cloned.1.call-update) | async-done | bytes 5242896 | tf_op jit(solution)/shard_map/all_gather | solution.py:50
  509.3 12.1 %gather_fusion.1 = f32[120,128,256]{2,1,0:T(8,128)} fusion(f32[40,128,256]{2,1,0:T(8,128)} %bitcast.167, s32[1024]{0:T(1024)S(1)} %pad_clamp_fusion), kind=kCustom, calls=%fused_computation.1 | custom fusion | bytes 31457760 | tf_op jit(solution)/shard_map/gather | solution.py:52
  521.4 20.2 %convolution_bitcast_fusion = f32[120,128,256]{1,2,0:T(8,128)} fusion(f32[120,128,256]{2,1,0:T(8,128)} %gather_fusion.1, bf16[120,128,128]{2,1,0:T(8,128)(2,1)} %param.8), kind=kOutput, calls=%fused_computation.10 | convolution fusion | flops 6039797760 | bytes 35389440 | tf_op jit(solution)/shard_map/sij,sjk->sik/dot_general | solution.py:53
  541.6 15.7 %copy.42 = f32[15,8,128,256]{3,1,2,0:T(8,128)} copy(f32[15,8,128,256]{2,3,1,0:T(8,128)} %bitcast.165) | data formatting | bytes 31457280
  557.3 11.6 %fusion.51 = f32[20,32768]{1,0:T(8,128)} fusion(f32[120,32768]{1,0:T(8,128)} %bitcast.162, f32[120]{0:T(128)S(1)} %compare_convert_fusion, s32[120]{0:T(128)S(1)} %copy-done.2), kind=kOutput, calls=%fused_computation.109 | convolution fusion | flops 943723200 | bytes 18351040 | tf_op jit(solution)/shard_map/dot_general | solution.py:56
  568.9 78.6 %fusion.1 = f32[8,32768]{1,0:T(8,128)S(1)} fusion(f32[20,32768]{1,0:T(8,128)} %fusion.51), kind=kCustom, calls=%all-reduce-scatter.1 | all-reduce-scatter fusion | flops 1048577 | bytes 3670528
  647.4 2.3 collective-permute-start.2
  653.4 19.9 %collective-permute-done.3 = f32[1,32768]{1,0:T(1,128)S(1)} collective-permute-done((f32[1,32768]{1,0:T(1,128)S(1)}, f32[1,32768]{1,0:T(1,128)S(1)}, u32[]{:S(2)}, u32[]{:S(2)}) %collective-permute-start.3) | collective-permute-done | bytes 131104
  673.3 21.2 %concatenate.4 = f32[17,32768]{1,0:T(8,128)} concatenate(f32[1,32768]{1,0:T(1,128)S(1)} %collective-permute-done.3, f32[8,32768]{1,0:T(8,128)} %collective-permute-done.2, f32[8,32768]{1,0:T(8,128)S(1)} %fusion.1), dimensions={0} | concatenate | bytes 4456448
  696.6 2.1 fusion.30
  698.8 131.3 %all-reduce.18.cloned.1.call-done = (f32[256,256]{0,1:T(8,128)}, f32[256,256]{1,0:T(8,128)}) async-done(((f32[256,256]{0,1:T(8,128)}, f32[256,256]{1,0:T(8,128)}), (f32[256,256]{0,1:T(8,128)}, f32[256,256]{1,0:T(8,128)})) %all-reduce.18.cloned.1.call-update) | async-done | bytes 524304 | tf_op jit(solution)/shard_map/psum | solution.py:68
  832.2 11.7 %cholesky.248 = f32[128,128]{1,0:T(8,128)S(1)} custom-call(f32[128,128]{1,0:T(8,128)S(1)} %cholesky.349), custom_call_target="Cholesky" | custom-call | tf_op jit(solution)/shard_map/jit(cholesky)/cholesky | solution.py:15
  844.0 9.8 custom-call.19
  854.3 11.7 %cholesky.265 = f32[128,128]{1,0:T(8,128)S(1)} custom-call(f32[128,128]{1,0:T(8,128)S(1)} %convolution_subtract_fusion.6), custom_call_target="Cholesky" | custom-call | tf_op jit(solution)/shard_map/jit(cholesky)/cholesky | solution.py:15
  868.7 4.0 while.9
  872.7 19.8 %custom-call.20 = f32[2,128,128]{1,2,0:T(8,128)S(1)} custom-call(f32[2,128,128]{2,1,0:T(8,128)S(1)} %get-tuple-element.31), custom_call_target="InvertDiagBlocksLowerTriangular" | custom-call | tf_op jit(solution)/shard_map/jit(_solve_triangular)/triangular_solve | solution.py:16
  895.2 11.7 %cholesky.282 = f32[128,128]{1,0:T(8,128)S(1)} custom-call(f32[128,128]{1,0:T(8,128)S(1)} %cholesky.352), custom_call_target="Cholesky" | custom-call | tf_op jit(solution)/shard_map/jit(cholesky)/cholesky | solution.py:15
  907.0 9.8 custom-call.21
  917.3 11.9 %cholesky.299 = f32[128,128]{1,0:T(8,128)S(1)} custom-call(f32[128,128]{1,0:T(8,128)S(1)} %convolution_subtract_fusion.5), custom_call_target="Cholesky" | custom-call | tf_op jit(solution)/shard_map/jit(cholesky)/cholesky | solution.py:15
  931.8 4.0 while.10
  935.8 19.7 %custom-call.22 = f32[2,128,128]{1,2,0:T(8,128)S(1)} custom-call(f32[2,128,128]{2,1,0:T(8,128)S(1)} %get-tuple-element.32), custom_call_target="InvertDiagBlocksLowerTriangular" | custom-call | tf_op jit(solution)/shard_map/jit(_solve_triangular)/triangular_solve | solution.py:16
  957.2 1.9 fusion.83
  959.2 34.7 %all-reduce.14.cloned.1.call-done = f32[256,256]{0,1:T(8,128)} async-done(((f32[256,256]{0,1:T(8,128)}), f32[256,256]{0,1:T(8,128)}) %all-reduce.14.cloned.1.call-update) | async-done | bytes 262160 | tf_op jit(solution)/shard_map/psum | solution.py:83
  995.1 55.5 %all-reduce.16.cloned.1.call-done = f32[256,256]{0,1:T(8,128)} async-done(((f32[256,256]{0,1:T(8,128)}), f32[256,256]{0,1:T(8,128)}) %all-reduce.16.cloned.1.call-update) | async-done | bytes 262160 | tf_op jit(solution)/shard_map/psum | solution.py:83
  1052.6 11.7 %cholesky.316 = f32[128,128]{1,0:T(8,128)S(1)} custom-call(f32[128,128]{1,0:T(8,128)S(1)} %cholesky.355), custom_call_target="Cholesky" | custom-call | tf_op jit(solution)/shard_map/jit(cholesky)/cholesky | solution.py:15
  1064.4 9.8 custom-call.23
  1074.7 11.7 %cholesky.333 = f32[128,128]{1,0:T(8,128)S(1)} custom-call(f32[128,128]{1,0:T(8,128)S(1)} %convolution_subtract_fusion.4), custom_call_target="Cholesky" | custom-call | tf_op jit(solution)/shard_map/jit(cholesky)/cholesky | solution.py:15
  1089.2 4.4 while.11
  1093.6 19.7 %custom-call.24 = f32[2,128,128]{1,2,0:T(8,128)S(1)} custom-call(f32[2,128,128]{2,1,0:T(8,128)S(1)} %get-tuple-element.33), custom_call_target="InvertDiagBlocksLowerTriangular" | custom-call | tf_op jit(solution)/shard_map/jit(_solve_triangular)/triangular_solve | solution.py:16
  (130 shorter events, 52.8 us)
Async XLA Ops:
  7.2 29.4 %copy-start.3 = (s32[120]{0:T(128)S(1)}, s32[120]{0:T(128)}, u32[]{:S(2)}) copy-start(s32[120]{0:T(128)} %param.10) | copy-start | bytes 1444
  7.2 68.7 %all-gather.3.cloned.1.call-start = ((), (), s32[]{:S(2)}) async-start(), calls=%async_computation | async-start | bytes 5898240 | tf_op jit(solution)/shard_map/all_gather | solution.py:50
  36.5 357.1 %all-reduce.12.cloned.1.call-start = ((), (), s32[]{:S(2)}) async-start(), calls=%async_computation.1 | async-start | bytes 524288 | tf_op jit(solution)/shard_map/psum | solution.py:65
  108.2 15.7 %copy-start.2 = (s32[120]{0:T(128)S(1)}, s32[120]{0:T(128)}, u32[]{:S(2)}) copy-start(s32[120]{0:T(128)} %param.9) | copy-start | bytes 1444
  212.9 49.5 %copy-start = (f32[640,256]{1,0:T(8,128)S(1)}, f32[640,256]{1,0:T(8,128)}, u32[]{:S(2)}) copy-start(f32[640,256]{1,0:T(8,128)} %param.12) | copy-start | bytes 1966084
  212.9 26.2 %collective-permute-start = (f32[8,32768]{1,0:T(8,128)}, f32[8,32768]{1,0:T(8,128)S(1)}, u32[]{:S(2)}, u32[]{:S(2)}) collective-permute-start(f32[8,32768]{1,0:T(8,128)} %fusion), channel_id=1, source_target_pairs={{0,8},{8,16},{16,24},{1,9},{9,17},{17,25},{2,10},{10,18},{18,26},{... | collective-permute-start | bytes 3145736
  215.7 23.4 %collective-permute-start.1 = (f32[1,32768]{1,0:T(1,128)S(1)}, f32[1,32768]{1,0:T(1,128)S(1)}, u32[]{:S(2)}, u32[]{:S(2)}) collective-permute-start(f32[1,32768]{1,0:T(1,128)S(1)} %slice.54), channel_id=1, source_target_pairs={{0,16},{8,24},{1,17},{9,25},{2,18},{10,26},{3,19},{11,27},{4,20},{... | collective-permute-start | bytes 393224
  264.6 244.7 %all-gather.5.cloned.1.call-start = ((), (), s32[]{:S(2)}) async-start(), calls=%async_computation.2 | async-start | bytes 5898240 | tf_op jit(solution)/shard_map/all_gather | solution.py:50
  469.1 361.0 %all-reduce.18.cloned.1.call-start = ((), (), s32[]{:S(2)}) async-start(), calls=%async_computation.5 | async-start | bytes 1048576 | tf_op jit(solution)/shard_map/psum | solution.py:68
  647.4 25.9 %collective-permute-start.2 = (f32[8,32768]{1,0:T(8,128)S(1)}, f32[8,32768]{1,0:T(8,128)}, u32[]{:S(2)}, u32[]{:S(2)}) collective-permute-start(f32[8,32768]{1,0:T(8,128)S(1)} %fusion.1), channel_id=1, source_target_pairs={{0,8},{8,16},{16,24},{1,9},{9,17},{17,25},{2,10},{10,18},{18,26},{... | collective-permute-start | bytes 3145736
  649.8 23.5 %collective-permute-start.3 = (f32[1,32768]{1,0:T(1,128)S(1)}, f32[1,32768]{1,0:T(1,128)S(1)}, u32[]{:S(2)}, u32[]{:S(2)}) collective-permute-start(f32[1,32768]{1,0:T(1,128)S(1)} %slice.55), channel_id=1, source_target_pairs={{0,16},{8,24},{1,17},{9,25},{2,18},{10,26},{3,19},{11,27},{4,20},{... | collective-permute-start | bytes 393224
  698.7 295.1 %all-reduce.14.cloned.1.call-start = ((), (), s32[]{:S(2)}) async-start(), calls=%async_computation.3 | async-start | bytes 524288 | tf_op jit(solution)/shard_map/psum | solution.py:83
  830.1 64.1 %copy-start.1 = (f32[256,256]{1,0:T(8,128)S(1)}, f32[256,256]{1,0:T(8,128)}, u32[]{:S(2)}) copy-start(f32[256,256]{1,0:T(8,128)} %get-tuple-element.67) | copy-start | bytes 786436
  959.1 91.4 %all-reduce.16.cloned.1.call-start = ((), (), s32[]{:S(2)}) async-start(), calls=%async_computation.4 | async-start | bytes 524288 | tf_op jit(solution)/shard_map/psum | solution.py:83
Sparse Core Ops, SparseCore 0:
  36.7 39.1 all-gather.2
  264.7 128.9 all-reduce.11
  469.2 40.0 all-gather.4
  698.9 131.1 all-reduce.17
  959.2 34.5 all-reduce.13
  996.8 53.7 all-reduce.15
